TPU v7x, 128 devices: a whole 4x4x4 slice. The times are simulated.
128 devices in a mesh: dp: 8 (over z, core), mp: 16 (over x, y).
Axes of the slice: x: 4, y: 4, z: 4, core: 2. Of those that a mesh axis runs over, the one named last changes fastest.
Arguments:
- tokens: bfloat16 [8192, 4096], P('dp', 'mp'), parts along dimension 0, may hold values from -6 to 6
- cotangent: bfloat16 [8192, 4096], P('dp', 'mp'), parts along dimension 0, may hold values from -6 to 6
- offsets: int32 [64], P('dp'), parts along dimension 0, may hold values from 0 to 960, as said below
- w_gate: bfloat16 [4096, 14336], P(None, 'mp'), may hold values from -0.09375 to 0.09375
- w_up: bfloat16 [4096, 14336], P(None, 'mp'), may hold values from -0.09375 to 0.09375
- w_down: bfloat16 [14336, 4096], P('mp'), may hold values from -0.046875 to 0.046875
- feature_proj: bfloat16 [4096, 192], replicated, may hold values from -0.09375 to 0.09375
- hidden_proj: bfloat16 [14336, 192], P('mp'), may hold values from -0.046875 to 0.046875
Outputs:
- input_grad: bfloat16 [4096, 4096], P(('dp', 'mp')), parts along dimension 0
- projected_grads: float32 [3, 64, 64, 64], P(None, 'dp'), parts along dimension 1
There are 8 independent parts, one for each index of `dp`. A program takes and returns all parts, laid end to end along the dimension named above; an argument that names none is the same for every part. Nothing has to cross between parts.
Inputs may be any that keep to these rules, and one draw needn't show every extreme that they name: `offsets`: spans lie inside the batch and may intersect; in every draw some span starts at 0 and some at 960.
All inputs are finite; a program needn't handle non-finite values.
Results may differ from a plain program's by a relative error of at most 0.0049.
Values may be sent and summed in bfloat16 or wider, within the bound.
No kernel may reach another device: no remote copies, remote signals or barrier semaphores. Data moves between devices by JAX's collectives and lax.ppermute only.
A program may use at most 128 MiB of HBM per device.

v0:
```python
import jax
import jax.numpy as jnp
from jax import lax
from jax.sharding import PartitionSpec as P

RANK = 64
SPAN_LEN = 64


def per_device(tokens, cotangent, offsets, w_gate, w_up, w_down, feature_proj, hidden_proj):
    positions = (offsets[:, None] + jnp.arange(SPAN_LEN, dtype=jnp.int32)[None, :]).reshape(-1)
    span_rows = positions.shape[0]
    span_x = jnp.take(lax.all_gather(tokens, "mp", axis=1, tiled=True), positions, axis=0)
    span_g = jnp.take(lax.all_gather(cotangent, "mp", axis=1, tiled=True), positions, axis=0)
    sums = (
        jnp.dot(span_x, w_gate, preferred_element_type=jnp.float32),
        jnp.dot(span_x, w_up, preferred_element_type=jnp.float32),
        jnp.einsum("td,fd->tf", span_g, w_down, preferred_element_type=jnp.float32),
        jnp.dot(span_x, feature_proj, preferred_element_type=jnp.float32),
        jnp.dot(span_g, feature_proj, preferred_element_type=jnp.float32),
    )
    pre_gate, pre_up, grad_hidden, feat_x, feat_g = sums
    sigmoid_gate = jax.nn.sigmoid(pre_gate)
    activated = pre_gate * sigmoid_gate
    hidden = (activated * pre_up).astype(jnp.bfloat16)
    grad_gate = (
        grad_hidden * pre_up * sigmoid_gate * (1.0 + pre_gate * (1.0 - sigmoid_gate))
    ).astype(jnp.bfloat16)
    grad_up = (grad_hidden * activated).astype(jnp.bfloat16)
    span_count = span_rows // SPAN_LEN
    input_grad = lax.psum_scatter(
        jnp.einsum("tf,df->td", grad_gate, w_gate, preferred_element_type=jnp.float32)
        + jnp.einsum("tf,df->td", grad_up, w_up, preferred_element_type=jnp.float32),
        "mp",
        scatter_dimension=0,
        tiled=True,
    ).astype(jnp.bfloat16)
    hid_gate = jnp.dot(grad_gate, hidden_proj[:, :RANK], preferred_element_type=jnp.float32)
    hid_up = jnp.dot(grad_up, hidden_proj[:, RANK : 2 * RANK], preferred_element_type=jnp.float32)
    hid_down = jnp.dot(hidden, hidden_proj[:, 2 * RANK :], preferred_element_type=jnp.float32)
    hid_gate, hid_up, hid_down = lax.psum((hid_gate, hid_up, hid_down), "mp")

    def per_span(left, right):
        return jnp.einsum(
            "slr,slq->srq",
            left.reshape(span_count, SPAN_LEN, RANK),
            right.reshape(span_count, SPAN_LEN, RANK),
            precision=lax.Precision.HIGHEST,
        )

    projected_grads = jnp.stack(
        [
            per_span(feat_x[:, :RANK], hid_gate),
            per_span(feat_x[:, RANK : 2 * RANK], hid_up),
            per_span(hid_down, feat_g[:, 2 * RANK :]),
        ],
        axis=0,
    )
    return (input_grad, projected_grads)


def solution(mesh):
    in_specs = (
        P("dp", "mp"),
        P("dp", "mp"),
        P("dp"),
        P(None, "mp"),
        P(None, "mp"),
        P("mp", None),
        P(),
        P("mp", None),
    )
    out_specs = (P(("dp", "mp"), None), P(None, "dp", None, None))
    return jax.shard_map(
        per_device, mesh=mesh, in_specs=in_specs, out_specs=out_specs, check_vma=False
    )
```

profile of v0, /device:TPU:0, one launch (start us, length us, event | category | flops | bytes accessed | tf_op | source)
XLA Modules:
  0.0 387.4 jit_solution(1904337492347919827)
XLA Ops:
  7.2 0.0 all-gather.5.cloned.1.call-start
  7.2 0.7 all-gather.5.cloned.1.call-update
  7.9 0.0 all-gather.3.cloned.1.call-start
  7.9 0.7 all-gather.3.cloned.1.call-update
  8.6 0.0 all-reduce.3.cloned.1.call-start
  8.7 0.7 iota_add_fusion
  9.4 0.1 add.43
  9.5 80.2 %all-gather.5.cloned.1.call-done = bf16[1024,4096]{1,0:T(8,128)(2,1)} async-done(((bf16[1024,256]{1,0:T(8,128)(2,1)}), bf16[1024,4096]{1,0:T(8,128)(2,1)}) %all-gather.5.cloned.1.call-update) | async-done | bytes 8388624 | tf_op jit(solution)/shard_map/all_gather | solution.py:13
  89.7 13.0 %gather_fusion.1 = bf16[512,4096]{1,0:T(8,128)(2,1)} fusion(bf16[1024,4096]{1,0:T(8,128)(2,1)} %all-gather.5.cloned.1.call-done, s32[1024]{0:T(1024)S(1)} %pad_clamp_fusion), kind=kCustom, calls=%fused_computation.1.clone | custom fusion | bytes 8390656 | tf_op jit(solution)/shard_map/jit(_take)/gather | solution.py:13
  102.7 0.0 copy-start
  102.7 11.0 %fusion.18 = f32[512,896]{1,0:T(8,128)S(1)} fusion(bf16[4096,896]{1,0:T(8,128)(2,1)} %param.14, bf16[512,4096]{1,0:T(8,128)(2,1)} %gather_fusion.1, pred[512]{0:T(512)(128)(4,1)S(1)} %compare_and_fusion), kind=kOutput, calls=%fused_computation.34 | convolution fusion | flops 3760193536 | bytes 13369856 | tf_op jit(solution)/shard_map/dot_general | solution.py:17
  113.7 0.0 copy-done
  113.8 0.0 copy-start.1
  113.8 9.1 %fusion.17 = f32[512,896]{1,0:T(8,128)S(1)} fusion(bf16[4096,896]{1,0:T(8,128)(2,1)} %param.13, bf16[512,4096]{1,0:T(8,128)(2,1)S(1)} %copy-done, pred[512]{0:T(512)(128)(4,1)S(1)} %compare_and_fusion), kind=kOutput, calls=%fused_computation.33 | convolution fusion | flops 3760193536 | bytes 13369856 | tf_op jit(solution)/shard_map/dot_general | solution.py:16
  122.9 0.0 copy-start.3
  122.9 1.2 copy-done.3
  124.2 0.0 copy-done.1
  124.2 0.7 fusion.3
  124.8 43.5 %all-gather.3.cloned.1.call-done = bf16[1024,4096]{1,0:T(8,128)(2,1)} async-done(((bf16[1024,256]{1,0:T(8,128)(2,1)}), bf16[1024,4096]{1,0:T(8,128)(2,1)}) %all-gather.3.cloned.1.call-update) | async-done | bytes 8388624 | tf_op jit(solution)/shard_map/all_gather | solution.py:14
  168.3 13.2 %gather_fusion = bf16[512,4096]{1,0:T(8,128)(2,1)} fusion(bf16[1024,4096]{1,0:T(8,128)(2,1)} %all-gather.3.cloned.1.call-done, s32[1024]{0:T(1024)S(1)} %pad_clamp_fusion), kind=kCustom, calls=%fused_computation.clone | custom fusion | bytes 8390656 | tf_op jit(solution)/shard_map/jit(_take)/gather | solution.py:14
  181.5 9.8 %multiply_convert_fusion.1 = (bf16[512,896]{1,0:T(8,128)(2,1)S(1)}, bf16[512,896]{1,0:T(8,128)(2,1)S(1)}) fusion(f32[512,896]{1,0:T(8,128)} %copy-done.3, f32[512,896]{1,0:T(8,128)S(1)} %fusion.18, bf16[896,4096]{1,0:T(8,128)(2,1)} %param.15, bf16[512,4096]{1,0:T(8,128)(2,1)} %gather_fusion, pred[512]{0:T(512)(128)(4,1)S(1)} %compare_and_fusion), kind=kOutput, calls=%fused_computation.6 | convolution fusion | flops 3766157312 | bytes 17039872 | tf_op jit(solution)/shard_map/td,fd->tf/dot_general | solution.py:18
  191.4 1.1 fusion.11
  192.5 9.8 %fusion.20 = f32[512,4096]{1,0:T(8,128)} fusion(bf16[512,896]{1,0:T(8,128)(2,1)S(1)} %get-tuple-element.7, bf16[4096,896]{1,0:T(8,128)(2,1)} %param.13), kind=kOutput, calls=%fused_computation.36 | convolution fusion | flops 3758096384 | bytes 16646144 | tf_op jit(solution)/shard_map/tf,df->td/dot_general | solution.py:32
  202.3 1.1 fusion.9
  203.4 0.1 reshape.36
  203.5 0.8 copy.14
  204.2 0.0 all-reduce.3.cloned.1.call-update
  204.3 0.0 reduce-scatter.2.cloned.1.call-start
  204.3 11.3 %convolution_add_fusion = f32[512,4096]{1,0:T(8,128)} fusion(f32[512,4096]{1,0:T(8,128)} %fusion.20, bf16[512,896]{1,0:T(8,128)(2,1)S(1)} %get-tuple-element.6, bf16[4096,896]{1,0:T(8,128)(2,1)} %param.14), kind=kOutput, calls=%fused_computation.2 | convolution fusion | flops 3760193536 | bytes 25034752 | tf_op jit(solution)/shard_map/tf,df->td/dot_general | solution.py:33
  215.6 0.0 copy-start.2
  215.6 0.0 reduce-scatter.2.cloned.1.call-update
  215.6 1.4 copy-done.2
  217.0 3.9 %fusion.16 = f32[512,192]{0,1:T(8,128)S(1)} fusion(bf16[4096,192]{0,1:T(8,128)(2,1)S(1)} %copy-done.2, bf16[512,4096]{1,0:T(8,128)(2,1)} %gather_fusion.1, pred[512]{0:T(512)(128)(4,1)S(1)} %compare_and_fusion), kind=kOutput, calls=%fused_computation.32 | convolution fusion | flops 807403520 | bytes 6160896 | tf_op jit(solution)/shard_map/dot_general | solution.py:19
  221.0 0.1 reshape.32
  221.1 0.1 reshape.34
  221.2 3.5 fusion.1
  224.7 65.8 %all-reduce.3.cloned.1.call-done = (f32[8,64,64]{1,2,0:T(8,128)}, f32[8,64,64]{2,1,0:T(8,128)}, f32[8,64,64]{2,1,0:T(8,128)}) async-done(((f32[8,64,64]{1,2,0:T(8,128)}, f32[8,64,64]{2,1,0:T(8,128)}, f32[8,64,64]{2,1,0:T(8,128)}), (f32[8,64,64]{1,2,0:T(8,128)}, f32[8,64,64]{2,1,0:T(8,128)}, f32[8,64,64]{2,1,0:T(8,128)})) %all-reduce.3.cloned.1.call-update) | async-done | bytes 393232 | tf_op jit(solution)/shard_map/psum | solution.py:41
  290.5 1.3 convolution_bitcast_fusion.2
  291.8 1.4 convolution_bitcast_fusion.1
  293.2 1.3 convolution_bitcast_fusion
  294.5 0.9 pad_maximum_fusion
  295.5 83.6 %reduce-scatter.2.cloned.1.call-done = f32[32,4096]{1,0:T(8,128)} async-done(((f32[512,4096]{1,0:T(8,128)}), f32[32,4096]{1,0:T(8,128)}) %reduce-scatter.2.cloned.1.call-update) | async-done | bytes 524304 | tf_op jit(solution)/shard_map/reduce_scatter | solution.py:31
  379.1 1.8 convert_element_type.14
  (4 shorter events, 0.0 us)
Async XLA Ops:
  7.2 82.5 %all-gather.5.cloned.1.call-start = ((), (), s32[]{:S(2)}) async-start(), calls=%async_computation.2 | async-start | bytes 8912896 | tf_op jit(solution)/shard_map/all_gather | solution.py:13
  7.9 160.4 %all-gather.3.cloned.1.call-start = ((), (), s32[]{:S(2)}) async-start(), calls=%async_computation.1 | async-start | bytes 8912896 | tf_op jit(solution)/shard_map/all_gather | solution.py:14
  8.6 281.8 %all-reduce.3.cloned.1.call-start = ((), (), s32[]{:S(2)}) async-start(), calls=%async_computation.4 | async-start | bytes 1572864 | tf_op jit(solution)/shard_map/psum | solution.py:41
  102.7 11.0 %copy-start = (bf16[512,4096]{1,0:T(8,128)(2,1)S(1)}, bf16[512,4096]{1,0:T(8,128)(2,1)}, u32[]{:S(2)}) copy-start(bf16[512,4096]{1,0:T(8,128)(2,1)} %gather_fusion.1) | copy-start | bytes 12582916
  113.8 10.4 %copy-start.1 = (bf16[896,192]{0,1:T(8,128)(2,1)S(1)}, bf16[896,192]{0,1:T(8,128)(2,1)}, u32[]{:S(2)}) copy-start(bf16[896,192]{0,1:T(8,128)(2,1)} %param.17) | copy-start | bytes 1032196
  122.9 1.3 copy-start.3
  204.3 174.8 %reduce-scatter.2.cloned.1.call-start = ((), (), s32[]{:S(2)}) async-start(), calls=%async_computation.3 | async-start | bytes 8912896 | tf_op jit(solution)/shard_map/reduce_scatter | solution.py:31
  215.6 1.4 copy-start.2
Sparse Core Ops, SparseCore 0:
  10.1 79.5 all-gather.4
  91.8 76.4 all-gather.2
  204.4 86.0 all-reduce.2
  293.8 85.2 reduce-scatter.1
where the time goes:
time: 388 us; the launch traced here: 387 us
  waiting for transfers between devices  274 us (71%)
  matrix products  65.4 us (17%)
  local copies, waits for them, and re-layouts  30.1 us (8%)
  between operations  13.9 us (4%)
    reduce_scatter x1, waiting for transfers between devices, per_device(): lax.psum_scatter(jnp.einsum('tf,df->td', grad_gate, w_gate, preferred_ele...  83.6 us
    all_gather x1, waiting for transfers between devices, per_device(): lax.all_gather(tokens, 'mp', axis=1, tiled=True)  80.2 us
    psum x1, waiting for transfers between devices, per_device(): hid_gate, hid_up, hid_down = lax.psum((hid_gate, hid_up, hid_down), 'mp')  65.8 us
    all_gather x1, waiting for transfers between devices, per_device(): lax.all_gather(cotangent, 'mp', axis=1, tiled=True)  43.5 us
    gather x1, local copies, waits for them, and re-layouts, per_device(): jnp.take(lax.all_gather(cotangent, 'mp', axis=1, tiled=True), positions,...  13.2 us
    gather x1, local copies, waits for them, and re-layouts, per_device(): jnp.take(lax.all_gather(tokens, 'mp', axis=1, tiled=True), positions, axi...  13 us
    dot_general x1, matrix products, per_device(): jnp.einsum('tf,df->td', grad_up, w_up, preferred_element_type=jnp.float32)  11.3 us
    dot_general x1, matrix products, per_device(): jnp.dot(span_x, w_up, preferred_element_type=jnp.float32)  11 us
  transfers between devices with their start and end apart: 4, of which 4 were waited for; matrix products, arithmetic and copies ran while one was open for 15% of the time, Pallas kernels for 0%

commit v1 on v0

--- a/solution.py
+++ b/solution.py
@@ -10,7 +10,7 @@
 def per_device(tokens, cotangent, offsets, w_gate, w_up, w_down, feature_proj, hidden_proj):
     positions = (offsets[:, None] + jnp.arange(SPAN_LEN, dtype=jnp.int32)[None, :]).reshape(-1)
     span_rows = positions.shape[0]
-    span_x = jnp.take(lax.all_gather(tokens, "mp", axis=1, tiled=True), positions, axis=0)
+    span_x = jnp.take(jnp.concatenate(lax.all_gather(tokens, "mp"), axis=1), positions, axis=0)
     span_g = jnp.take(lax.all_gather(cotangent, "mp", axis=1, tiled=True), positions, axis=0)
     sums = (
         jnp.dot(span_x, w_gate, preferred_element_type=jnp.float32),

time: 388 us -> 382 us (0.985)
  waiting for transfers between devices: 274 us -> 261 us
  local copies, waits for them, and re-layouts: 30.1 us -> 37.9 us
    unnamed x8 -> x9, local copies, waits for them, and re-layouts: 2.64 us -> 10.4 us
    all_gather x1, waiting for transfers between devices: 43.5 us -> 36 us  [per_device(): lax.all_gather(cotangent, 'mp', axis=1, tiled=True)]
    all_gather x1, waiting for transfers between devices: 80.2 us -> 73.8 us  [per_device(): lax.all_gather(tokens, 'mp')]
  transfers between devices with their start and end apart: 4 -> 4, of which waited for: 4 -> 4; matrix products, arithmetic and copies ran while one was open for 15% -> 17% of each run, Pallas kernels for 0% -> 0%
where the time goes in v1:
time: 382 us; the launch traced here: 381 us
  waiting for transfers between devices  261 us (68%)
  matrix products  65.5 us (17%)
  local copies, waits for them, and re-layouts  37.9 us (10%)
  between operations  13.9 us (4%)
    reduce_scatter x1, waiting for transfers between devices, per_device(): lax.psum_scatter(jnp.einsum('tf,df->td', grad_gate, w_gate, preferred_ele...  83.6 us
    all_gather x1, waiting for transfers between devices, per_device(): lax.all_gather(tokens, 'mp')  73.8 us
    psum x1, waiting for transfers between devices, per_device(): hid_gate, hid_up, hid_down = lax.psum((hid_gate, hid_up, hid_down), 'mp')  65.8 us
    all_gather x1, waiting for transfers between devices, per_device(): lax.all_gather(cotangent, 'mp', axis=1, tiled=True)  36 us
    gather x1, local copies, waits for them, and re-layouts, per_device(): jnp.take(lax.all_gather(cotangent, 'mp', axis=1, tiled=True), positions,...  13.2 us
    gather x1, local copies, waits for them, and re-layouts, per_device(): jnp.take(jnp.concatenate(lax.all_gather(tokens, 'mp'), axis=1), positions...  13.1 us
    dot_general x1, matrix products, per_device(): jnp.einsum('tf,df->td', grad_up, w_up, preferred_element_type=jnp.float32)  11.3 us
    dot_general x1, matrix products, per_device(): jnp.dot(span_x, w_up, preferred_element_type=jnp.float32)  11 us
  transfers between devices with their start and end apart: 4, of which 4 were waited for; matrix products, arithmetic and copies ran while one was open for 17% of the time, Pallas kernels for 0%

profile of v1, /device:TPU:0, one launch (start us, length us, event | category | flops | bytes accessed | tf_op | source)
XLA Modules:
  0.0 381.4 jit_solution(14263999553083885390)
XLA Ops:
  7.2 0.0 all-gather.6.cloned.1.call-start
  7.2 0.7 all-gather.6.cloned.1.call-update
  7.9 0.0 all-gather.4.cloned.1.call-start
  7.9 0.7 all-gather.4.cloned.1.call-update
  8.6 0.0 all-reduce.3.cloned.1.call-start
  8.7 0.7 iota_add_fusion
  9.4 0.1 add.43
  9.5 73.8 %all-gather.6.cloned.1.call-done = bf16[16384,256]{1,0:T(8,128)(2,1)} async-done(((bf16[1024,256]{1,0:T(8,128)(2,1)}), bf16[16384,256]{1,0:T(8,128)(2,1)}) %all-gather.6.cloned.1.call-update) | async-done | bytes 8388624 | tf_op jit(solution)/shard_map/all_gather | solution.py:13
  83.3 7.8 %copy.20 = bf16[128,8,16,256]{3,1,2,0:T(8,128)(2,1)} copy(bf16[128,8,16,256]{3,1,0,2:T(8,128)(2,1)} %bitcast.36) | data formatting | bytes 16777216
  91.1 13.1 %gather_fusion.1 = bf16[512,4096]{1,0:T(8,128)(2,1)} fusion(bf16[1024,4096]{1,0:T(8,128)(2,1)} %bitcast.35, s32[1024]{0:T(1024)S(1)} %pad_clamp_fusion), kind=kCustom, calls=%fused_computation.1.clone | custom fusion | bytes 8390656 | tf_op jit(solution)/shard_map/jit(_take)/gather | solution.py:13
  104.1 0.0 copy-start
  104.1 11.0 %fusion.18 = f32[512,896]{1,0:T(8,128)S(1)} fusion(bf16[4096,896]{1,0:T(8,128)(2,1)} %param.14, bf16[512,4096]{1,0:T(8,128)(2,1)} %gather_fusion.1, pred[512]{0:T(512)(128)(4,1)S(1)} %compare_and_fusion), kind=kOutput, calls=%fused_computation.34 | convolution fusion | flops 3760193536 | bytes 13369856 | tf_op jit(solution)/shard_map/dot_general | solution.py:17
  115.2 0.0 copy-done
  115.2 0.0 copy-start.1
  115.2 9.1 %fusion.17 = f32[512,896]{1,0:T(8,128)S(1)} fusion(bf16[4096,896]{1,0:T(8,128)(2,1)} %param.13, bf16[512,4096]{1,0:T(8,128)(2,1)S(1)} %copy-done, pred[512]{0:T(512)(128)(4,1)S(1)} %compare_and_fusion), kind=kOutput, calls=%fused_computation.33 | convolution fusion | flops 3760193536 | bytes 13369856 | tf_op jit(solution)/shard_map/dot_general | solution.py:16
  124.3 0.0 copy-start.3
  124.3 1.3 copy-done.3
  125.6 0.0 copy-done.1
  125.6 0.7 fusion.3
  126.3 36.0 %all-gather.4.cloned.1.call-done = bf16[1024,4096]{1,0:T(8,128)(2,1)} async-done(((bf16[1024,256]{1,0:T(8,128)(2,1)}), bf16[1024,4096]{1,0:T(8,128)(2,1)}) %all-gather.4.cloned.1.call-update) | async-done | bytes 8388624 | tf_op jit(solution)/shard_map/all_gather | solution.py:14
  162.2 13.2 %gather_fusion = bf16[512,4096]{1,0:T(8,128)(2,1)} fusion(bf16[1024,4096]{1,0:T(8,128)(2,1)} %all-gather.4.cloned.1.call-done, s32[1024]{0:T(1024)S(1)} %pad_clamp_fusion), kind=kCustom, calls=%fused_computation.clone | custom fusion | bytes 8390656 | tf_op jit(solution)/shard_map/jit(_take)/gather | solution.py:14
  175.4 9.9 %multiply_convert_fusion.1 = (bf16[512,896]{1,0:T(8,128)(2,1)S(1)}, bf16[512,896]{1,0:T(8,128)(2,1)S(1)}) fusion(f32[512,896]{1,0:T(8,128)} %copy-done.3, f32[512,896]{1,0:T(8,128)S(1)} %fusion.18, bf16[896,4096]{1,0:T(8,128)(2,1)} %param.15, bf16[512,4096]{1,0:T(8,128)(2,1)} %gather_fusion, pred[512]{0:T(512)(128)(4,1)S(1)} %compare_and_fusion), kind=kOutput, calls=%fused_computation.6 | convolution fusion | flops 3766157312 | bytes 17039872 | tf_op jit(solution)/shard_map/td,fd->tf/dot_general | solution.py:18
  185.3 1.1 fusion.11
  186.4 9.8 %fusion.20 = f32[512,4096]{1,0:T(8,128)} fusion(bf16[512,896]{1,0:T(8,128)(2,1)S(1)} %get-tuple-element.7, bf16[4096,896]{1,0:T(8,128)(2,1)} %param.13), kind=kOutput, calls=%fused_computation.36 | convolution fusion | flops 3758096384 | bytes 16646144 | tf_op jit(solution)/shard_map/tf,df->td/dot_general | solution.py:32
  196.3 1.1 fusion.9
  197.3 0.1 reshape.44
  197.5 0.8 copy.15
  198.2 0.0 all-reduce.3.cloned.1.call-update
  198.2 0.0 reduce-scatter.2.cloned.1.call-start
  198.3 11.3 %convolution_add_fusion = f32[512,4096]{1,0:T(8,128)} fusion(f32[512,4096]{1,0:T(8,128)} %fusion.20, bf16[512,896]{1,0:T(8,128)(2,1)S(1)} %get-tuple-element.6, bf16[4096,896]{1,0:T(8,128)(2,1)} %param.14), kind=kOutput, calls=%fused_computation.2 | convolution fusion | flops 3760193536 | bytes 25034752 | tf_op jit(solution)/shard_map/tf,df->td/dot_general | solution.py:33
  209.6 0.0 copy-start.2
  209.6 0.0 reduce-scatter.2.cloned.1.call-update
  209.6 1.4 copy-done.2
  211.0 3.9 %fusion.16 = f32[512,192]{0,1:T(8,128)S(1)} fusion(bf16[4096,192]{0,1:T(8,128)(2,1)S(1)} %copy-done.2, bf16[512,4096]{1,0:T(8,128)(2,1)} %gather_fusion.1, pred[512]{0:T(512)(128)(4,1)S(1)} %compare_and_fusion), kind=kOutput, calls=%fused_computation.32 | convolution fusion | flops 807403520 | bytes 6160896 | tf_op jit(solution)/shard_map/dot_general | solution.py:19
  214.9 0.1 reshape.40
  215.0 0.1 reshape.42
  215.1 3.5 fusion.1
  218.7 65.8 %all-reduce.3.cloned.1.call-done = (f32[8,64,64]{1,2,0:T(8,128)}, f32[8,64,64]{2,1,0:T(8,128)}, f32[8,64,64]{2,1,0:T(8,128)}) async-done(((f32[8,64,64]{1,2,0:T(8,128)}, f32[8,64,64]{2,1,0:T(8,128)}, f32[8,64,64]{2,1,0:T(8,128)}), (f32[8,64,64]{1,2,0:T(8,128)}, f32[8,64,64]{2,1,0:T(8,128)}, f32[8,64,64]{2,1,0:T(8,128)})) %all-reduce.3.cloned.1.call-update) | async-done | bytes 393232 | tf_op jit(solution)/shard_map/psum | solution.py:41
  284.5 1.3 convolution_bitcast_fusion.2
  285.8 1.4 convolution_bitcast_fusion.1
  287.2 1.3 convolution_bitcast_fusion
  288.5 0.9 pad_maximum_fusion
  289.4 83.6 %reduce-scatter.2.cloned.1.call-done = f32[32,4096]{1,0:T(8,128)} async-done(((f32[512,4096]{1,0:T(8,128)}), f32[32,4096]{1,0:T(8,128)}) %reduce-scatter.2.cloned.1.call-update) | async-done | bytes 524304 | tf_op jit(solution)/shard_map/reduce_scatter | solution.py:31
  373.1 1.8 convert_element_type.14
  (4 shorter events, 0.0 us)
Async XLA Ops:
  7.2 76.1 %all-gather.6.cloned.1.call-start = ((), (), s32[]{:S(2)}) async-start(), calls=%async_computation.3 | async-start | bytes 8912896 | tf_op jit(solution)/shard_map/all_gather | solution.py:13
  7.9 154.3 %all-gather.4.cloned.1.call-start = ((), (), s32[]{:S(2)}) async-start(), calls=%async_computation.1 | async-start | bytes 8912896 | tf_op jit(solution)/shard_map/all_gather | solution.py:14
  8.6 275.8 %all-reduce.3.cloned.1.call-start = ((), (), s32[]{:S(2)}) async-start(), calls=%async_computation.4 | async-start | bytes 1572864 | tf_op jit(solution)/shard_map/psum | solution.py:41
  104.1 11.0 %copy-start = (bf16[512,4096]{1,0:T(8,128)(2,1)S(1)}, bf16[512,4096]{1,0:T(8,128)(2,1)}, u32[]{:S(2)}) copy-start(bf16[512,4096]{1,0:T(8,128)(2,1)} %gather_fusion.1) | copy-start | bytes 12582916
  115.2 10.4 %copy-start.1 = (bf16[896,192]{0,1:T(8,128)(2,1)S(1)}, bf16[896,192]{0,1:T(8,128)(2,1)}, u32[]{:S(2)}) copy-start(bf16[896,192]{0,1:T(8,128)(2,1)} %param.17) | copy-start | bytes 1032196
  124.3 1.3 copy-start.3
  198.2 174.8 %reduce-scatter.2.cloned.1.call-start = ((), (), s32[]{:S(2)}) async-start(), calls=%async_computation.2 | async-start | bytes 8912896 | tf_op jit(solution)/shard_map/reduce_scatter | solution.py:31
  209.6 1.4 copy-start.2
Sparse Core Ops, SparseCore 0:
  10.1 73.1 all-gather.5
  85.4 76.7 all-gather.3
  198.3 86.0 all-reduce.2
  287.7 85.2 reduce-scatter.1
